TPU v7x, 256 devices: a whole 4x4x8 slice. The times are simulated.
256 devices in a mesh: row: 16 (over y_lo, x, core), col: 16 (over y_hi, z).
Axes of the slice: x: 4, y: 4 (y_hi: 2, y_lo: 2; y = y_hi * 2 + y_lo), z: 8, core: 2. Of those that a mesh axis runs over, the one named last changes fastest.
Arguments:
- val_orb: bfloat16 [64, 2048], replicated, may hold values from -6 to 6
- con_orb: bfloat16 [512, 2048], replicated, may hold values from -6 to 6
- val_energy: float32 [64], replicated, may hold values from -1.5 to -0.5
- con_energy: float32 [512], replicated, may hold values from 0.5 to 2
- points: int32 [1024], replicated, may hold values from 0 to 2047, as said below
- val_band: int32 [1048576], P(('row', 'col')), may hold values from 0 to 63
- con_band: int32 [1048576], P(('row', 'col')), may hold values from 0 to 511
- kernel: bfloat16 [1024, 1024], replicated
- trial_vecs: bfloat16 [1048576, 128], P(('row', 'col')), may hold values from -6 to 6
Outputs:
- first_degree: bfloat16 [1048576, 128], P(('row', 'col'))
- filtered: float32 [1048576, 128], P(('row', 'col'))
Inputs may be any that keep to these rules, and one draw needn't show every extreme that they name: Distinct grid points.
All inputs are finite; a program needn't handle non-finite values.
Results may differ from a plain program's by a relative error of at most 0.0042.
Values sent between devices are 32-bit elements; how exact they have to be, the bound alone decides.
A program may use at most 128 MiB of HBM per device.

v0:
```python
import jax
import jax.numpy as jnp
from jax import lax
from jax.sharding import PartitionSpec as P

filter_center = 2.25
filter_half = 1.25


def factor_rows(val_points, con_points, val_band, con_band):
    product = jnp.take(val_points, val_band, axis=0).astype(jnp.float32) * jnp.take(
        con_points, con_band, axis=0
    ).astype(jnp.float32)
    return product.astype(jnp.bfloat16)


def shards(
    val_orb, con_orb, val_energy, con_energy, points, val_band, con_band, kernel, trial_vecs
):
    val_points = jnp.take(val_orb, points, axis=1)
    con_points = jnp.take(con_orb, points, axis=1)
    energy = (jnp.take(con_energy, con_band) - jnp.take(val_energy, val_band))[:, None]
    own_rows = factor_rows(val_points, con_points, val_band, con_band)
    kernel_wide = kernel.astype(jnp.float32)
    rows_wide = own_rows.astype(jnp.float32)

    def apply_kernel(vectors):
        partial_proj = lax.dot_general(
            own_rows, vectors, (((0,), (0,)), ((), ())), preferred_element_type=jnp.float32
        )
        projected = lax.psum(partial_proj, ("row", "col"))
        mixed = jnp.dot(kernel_wide, projected, precision=lax.Precision.HIGHEST)
        return jnp.dot(rows_wide, mixed, precision=lax.Precision.HIGHEST)

    start_vecs = trial_vecs.astype(jnp.float32)
    first = ((energy - filter_center) * start_vecs + apply_kernel(trial_vecs)) / filter_half
    first_degree = first.astype(jnp.bfloat16)
    first_wide = first_degree.astype(jnp.float32)
    filtered = (
        2.0 * ((energy - filter_center) * first_wide + apply_kernel(first_degree)) / filter_half
        - start_vecs
    )
    return (first_degree, filtered)


def solution(mesh):
    placed = (
        P(),
        P(),
        P(),
        P(),
        P(),
        P(("row", "col")),
        P(("row", "col")),
        P(),
        P(("row", "col"), None),
    )
    return jax.shard_map(
        shards,
        mesh=mesh,
        in_specs=placed,
        out_specs=(P(("row", "col"), None), P(("row", "col"), None)),
        check_vma=False,
    )
```

profile of v0, /device:TPU:2, one launch (start us, length us, event | category | flops | bytes accessed | tf_op | source)
XLA Modules:
  0.0 709.2 jit_solution(5484198504451303308)
XLA Ops:
  7.2 0.0 copy-start
  7.2 0.0 all-reduce.3.cloned.1.call-start
  7.2 0.8 fusion.8
  8.1 0.7 compare_and_fusion.2
  8.8 1.6 fusion.12
  10.3 2.1 fusion.9
  12.4 2.1 fusion.10
  14.5 2.1 fusion.11
  16.6 1.3 fusion.7
  17.9 1.3 compare_and_fusion
  19.2 4.0 copy.17
  23.2 5.8 gather_fusion.3
  29.0 1.2 select_bitcast_fusion
  30.2 1.5 copy.18
  31.7 0.0 copy-done.11
  31.7 0.0 copy-done.5
  31.8 1.0 copy.15
  32.8 5.2 gather_fusion.1
  38.0 1.2 select_bitcast_fusion.1
  39.1 0.1 copy.16
  39.2 0.0 copy-start.1
  39.3 18.3 %gather_fusion.4 = bf16[4096,1024]{1,0:T(8,128)(2,1)} fusion(bf16[512,1024]{1,0:T(8,128)(2,1)S(1)} %copy.18, s32[4096]{0:T(1024)S(1)} %fusion.6), kind=kCustom, calls=%fused_computation.4 | custom fusion | bytes 16793600 | tf_op jit(solution)/shard_map/jit(_take)/gather | solution.py:11
  57.5 0.0 copy-done.1
  57.5 25.9 %gather_fusion = f32[4096]{0:T(1024)S(1)} fusion(f32[512]{0:T(512)S(1)} %copy-done.1, s32[4096]{0:T(1024)S(1)} %fusion.6), kind=kCustom, calls=%fused_computation | custom fusion | bytes 49152 | tf_op jit(solution)/shard_map/jit(_take)/gather | solution.py:22
  83.4 0.0 copy-start.6
  83.4 0.0 copy-start.9
  83.4 0.0 copy-start.10
  83.5 18.3 %gather_fusion.2 = bf16[4096,1024]{1,0:T(8,128)(2,1)} fusion(bf16[64,1024]{1,0:T(8,128)(2,1)S(1)} %copy.16, s32[4096]{0:T(1024)S(1)} %copy-done.7), kind=kCustom, calls=%fused_computation.2 | custom fusion | bytes 16793600 | tf_op jit(solution)/shard_map/jit(_take)/gather | solution.py:11
  101.7 0.0 copy-done.6
  101.7 40.1 %fusion.5 = (f32[4096]{0:T(1024)S(1)}, pred[4096]{0:T(1024)(128)(4,1)S(1)}) fusion(f32[4096]{0:T(1024)S(1)} %gather_fusion, s32[4096]{0:T(1024)S(1)} %copy-done.6, f32[]{:T(128)} %bitcast, f32[]{:T(128)} %bitcast.1, f32[]{:T(128)} %bitcast.2, f32[]{:T(128)} %bitcast.3, f32[]{:T(128)} %bitcast.4, f32[]{:T(128)} %bitcast.5, f32[]{:T(128)} %bitcast.6, ...), kind=kLoop, calls=%fused_computation.19 | loop fusion | flops 581632 | bytes 69888 | tf_op jit(solution)/shard_map/sub | solution.py:36
  141.8 0.0 copy-start.3
  141.8 7.7 %multiply_convert_fusion = bf16[4096,1024]{1,0:T(8,128)(2,1)S(1)} fusion(bf16[4096,1024]{1,0:T(8,128)(2,1)} %gather_fusion.4, bf16[4096,1024]{1,0:T(8,128)(2,1)} %gather_fusion.2, pred[4096]{0:T(1024)(128)(4,1)S(1)} %get-tuple-element.3, pred[4096]{0:T(1024)(128)(4,1)S(1)} %copy-done.10), kind=kLoop, calls=%fused_computation.5 | loop fusion | flops 25165824 | bytes 25174016 | tf_op jit(solution)/shard_map/convert_element_type | solution.py:14
  149.5 0.0 copy-start.2
  149.5 3.2 copy-done.2
  152.8 3.1 fusion.13
  155.9 0.0 all-reduce.3.cloned.1.call-update
  155.9 0.0 all-reduce.5.cloned.1.call-start
  156.0 258.4 %all-reduce.3.cloned.1.call-done = f32[1024,128]{1,0:T(8,128)} async-done(((f32[1024,128]{1,0:T(8,128)}), f32[1024,128]{1,0:T(8,128)}) %all-reduce.3.cloned.1.call-update) | async-done | bytes 524304 | tf_op jit(solution)/shard_map/psum | solution.py:31
  414.4 0.0 copy-done
  414.4 3.3 fusion.14
  417.8 9.3 %fusion.3 = bf16[4096,128]{1,0:T(8,128)(2,1)S(1)} fusion(bf16[4096,1024]{1,0:T(8,128)(2,1)} %copy-done.2, f32[128,1024]{1,0:T(8,128)S(1)} %fusion.14, bf16[4096,128]{1,0:T(8,128)(2,1)S(1)} %copy-done.3, f32[4096]{0:T(1024)S(1)} %get-tuple-element.2), kind=kOutput, calls=%fused_computation.11 | convolution fusion | flops 6445072384 | bytes 11026432 | tf_op jit(solution)/shard_map/dot_general | solution.py:33
  427.1 0.0 copy-start.4
  427.1 1.0 copy-done.4
  428.0 6.6 fusion.15
  434.6 0.0 all-reduce.5.cloned.1.call-update
  434.6 254.2 %all-reduce.5.cloned.1.call-done = f32[1024,128]{1,0:T(8,128)} async-done(((f32[1024,128]{1,0:T(8,128)}), f32[1024,128]{1,0:T(8,128)}) %all-reduce.5.cloned.1.call-update) | async-done | bytes 524304 | tf_op jit(solution)/shard_map/psum | solution.py:31
  688.8 3.3 fusion.16
  692.2 10.2 %fusion.1 = f32[4096,128]{1,0:T(8,128)} fusion(bf16[4096,1024]{1,0:T(8,128)(2,1)} %copy-done.2, f32[128,1024]{1,0:T(8,128)S(1)} %fusion.16, bf16[4096,128]{1,0:T(8,128)(2,1)S(1)} %copy-done.3, bf16[4096,128]{1,0:T(8,128)(2,1)} %copy-done.4, f32[4096]{0:T(1024)S(1)} %get-tuple-element.2), kind=kOutput, calls=%fused_computation.8 | convolution fusion | flops 6445596672 | bytes 13123584 | tf_op jit(solution)/shard_map/dot_general | solution.py:33
  (10 shorter events, 0.0 us)
Async XLA Ops:
  7.2 407.3 %copy-start = (bf16[1024,1024]{1,0:T(8,128)(2,1)S(1)}, bf16[1024,1024]{1,0:T(8,128)(2,1)}, u32[]{:S(2)}) copy-start(bf16[1024,1024]{1,0:T(8,128)(2,1)} %param.16) | copy-start | bytes 6291460
  7.2 407.3 %all-reduce.3.cloned.1.call-start = ((), (), s32[]{:S(2)}) async-start(), calls=%async_computation | async-start | bytes 1048576 | tf_op jit(solution)/shard_map/psum | solution.py:31
  8.8 23.0 %copy-start.11 = (pred[1024]{0:T(1024)(128)(4,1)}, pred[1024]{0:T(1024)(128)(4,1)S(1)}, u32[]{:S(2)}) copy-start(pred[1024]{0:T(1024)(128)(4,1)S(1)} %compare_and_fusion.2) | copy-start | bytes 3076
  19.2 12.5 %copy-start.8 = (s32[4096]{0:T(1024)S(1)}, s32[4096]{0:T(1024)}, u32[]{:S(2)}) copy-start(s32[4096]{0:T(1024)} %param.15) | copy-start | bytes 49156
  19.2 12.5 %copy-start.5 = (bf16[64,2048]{1,0:T(8,128)(2,1)S(1)}, bf16[64,2048]{1,0:T(8,128)(2,1)}, u32[]{:S(2)}) copy-start(bf16[64,2048]{1,0:T(8,128)(2,1)} %param.9) | copy-start | bytes 786436
  39.2 18.3 %copy-start.1 = (f32[512]{0:T(512)S(1)}, f32[512]{0:T(512)}, u32[]{:S(2)}) copy-start(f32[512]{0:T(512)} %param.12) | copy-start | bytes 6148
  57.5 25.9 %copy-start.7 = (s32[4096]{0:T(1024)S(1)}, s32[4096]{0:T(1024)}, u32[]{:S(2)}) copy-start(s32[4096]{0:T(1024)} %fusion.7) | copy-start | bytes 49156
  83.4 18.3 %copy-start.6 = (s32[4096]{0:T(1024)S(1)}, s32[4096]{0:T(1024)}, u32[]{:S(2)}) copy-start(s32[4096]{0:T(1024)} %param.14) | copy-start | bytes 49156
  83.4 18.3 %copy-start.9 = (s32[4096]{0:T(1024)S(1)}, s32[4096]{0:T(1024)}, u32[]{:S(2)}) copy-start(s32[4096]{0:T(1024)} %param.15) | copy-start | bytes 49156
  83.4 58.3 %copy-start.10 = (pred[4096]{0:T(1024)(128)(4,1)S(1)}, pred[4096]{0:T(1024)(128)(4,1)}, u32[]{:S(2)}) copy-start(pred[4096]{0:T(1024)(128)(4,1)} %compare_and_fusion) | copy-start | bytes 12292
  141.8 11.0 %copy-start.3 = (bf16[4096,128]{1,0:T(8,128)(2,1)S(1)}, bf16[4096,128]{1,0:T(8,128)(2,1)}, u32[]{:S(2)}) copy-start(bf16[4096,128]{1,0:T(8,128)(2,1)} %param.17) | copy-start | bytes 3145732
  149.5 3.2 copy-start.2
  155.9 532.9 %all-reduce.5.cloned.1.call-start = ((), (), s32[]{:S(2)}) async-start(), calls=%async_computation.1 | async-start | bytes 1048576 | tf_op jit(solution)/shard_map/psum | solution.py:31
  427.1 1.0 copy-start.4
Sparse Core Ops, SparseCore 0:
  156.1 258.3 all-reduce.2
  434.7 254.0 all-reduce.4
where the time goes:
time: 710 us; the launch traced here: 709 us
  waiting for transfers between devices  513 us (72%)
  local copies, waits for them, and re-layouts  92.1 us (13%)
  other arithmetic  54.3 us (8%)
  matrix products  35.8 us (5%)
  between operations  14.2 us (2%)
    psum x2, waiting for transfers between devices, apply_kernel(): projected = lax.psum(partial_proj, ('row', 'col'))  513 us
    sub x1, other arithmetic, shards(): energy - filter_center  40.1 us
    gather x1, local copies, waits for them, and re-layouts, shards(): jnp.take(con_energy, con_band) - jnp.take(val_energy, val_band)  25.9 us
    dot_general x2, matrix products, apply_kernel(): return jnp.dot(rows_wide, mixed, precision=lax.Precision.HIGHEST)  19.5 us
    gather x1, local copies, waits for them, and re-layouts, factor_rows(): jnp.take(con_points, con_band, axis=0).astype(jnp.float32)  18.3 us
    gather x1, local copies, waits for them, and re-layouts, factor_rows(): jnp.take(val_points, val_band, axis=0).astype(jnp.float32)  18.3 us
  transfers between devices with their start and end apart: 2, of which 2 were waited for; matrix products, arithmetic and copies ran while one was open for 0% of the time, Pallas kernels for 0%

commit v1 on v0

--- a/solution.py
+++ b/solution.py
@@ -28,7 +28,7 @@
         partial_proj = lax.dot_general(
             own_rows, vectors, (((0,), (0,)), ((), ())), preferred_element_type=jnp.float32
         )
-        projected = lax.psum(partial_proj, ("row", "col"))
+        projected = jax.lax.psum(jax.lax.psum(partial_proj, "row"), axis_name="col")
         mixed = jnp.dot(kernel_wide, projected, precision=lax.Precision.HIGHEST)
         return jnp.dot(rows_wide, mixed, precision=lax.Precision.HIGHEST)
 

time: 710 us -> 768 us (1.082)
  waiting for transfers between devices: 513 us -> 570 us
    psum x2 -> x4, waiting for transfers between devices: 513 us -> 570 us  [apply_kernel(): projected = jax.lax.psum(jax.lax.psum(partial_proj, 'row'), axis_name='col')]
  transfers between devices with their start and end apart: 2 -> 4, of which waited for: 2 -> 4; matrix products, arithmetic and copies ran while one was open for 0% -> 0% of each run, Pallas kernels for 0% -> 0%
where the time goes in v1:
time: 768 us; the launch traced here: 767 us
  waiting for transfers between devices  570 us (74%)
  local copies, waits for them, and re-layouts  92.1 us (12%)
  other arithmetic  54.3 us (7%)
  matrix products  35.6 us (5%)
  between operations  14 us (2%)
    psum x4, waiting for transfers between devices, apply_kernel(): projected = jax.lax.psum(jax.lax.psum(partial_proj, 'row'), axis_name='col')  570 us
    sub x1, other arithmetic, shards(): energy - filter_center  40.1 us
    gather x1, local copies, waits for them, and re-layouts, shards(): jnp.take(con_energy, con_band) - jnp.take(val_energy, val_band)  25.9 us
    dot_general x2, matrix products, apply_kernel(): return jnp.dot(rows_wide, mixed, precision=lax.Precision.HIGHEST)  19.3 us
    gather x1, local copies, waits for them, and re-layouts, factor_rows(): jnp.take(con_points, con_band, axis=0).astype(jnp.float32)  18.3 us
    gather x1, local copies, waits for them, and re-layouts, factor_rows(): jnp.take(val_points, val_band, axis=0).astype(jnp.float32)  18.3 us
  transfers between devices with their start and end apart: 4, of which 4 were waited for; matrix products, arithmetic and copies ran while one was open for 0% of the time, Pallas kernels for 0%

profile of v1, /device:TPU:2, one launch (start us, length us, event | category | flops | bytes accessed | tf_op | source)
XLA Modules:
  0.0 766.7 jit_solution(5335626166822628948)
XLA Ops:
  7.2 0.0 copy-start
  7.2 0.0 all-reduce.5.cloned.1.call-start
  7.2 0.8 fusion.8
  8.1 0.7 compare_and_fusion.2
  8.8 1.6 fusion.12
  10.3 2.1 fusion.9
  12.4 2.1 fusion.10
  14.5 2.1 fusion.11
  16.6 1.3 fusion.7
  17.9 1.3 compare_and_fusion
  19.2 4.0 copy.17
  23.2 5.8 gather_fusion.3
  29.0 1.2 select_bitcast_fusion
  30.2 1.5 copy.18
  31.7 0.0 copy-done.5
  31.8 1.0 copy.15
  32.8 5.2 gather_fusion.1
  38.0 1.2 select_bitcast_fusion.1
  39.1 0.1 copy.16
  39.2 0.0 copy-start.1
  39.3 18.3 %gather_fusion.4 = bf16[4096,1024]{1,0:T(8,128)(2,1)} fusion(bf16[512,1024]{1,0:T(8,128)(2,1)S(1)} %copy.18, s32[4096]{0:T(1024)S(1)} %fusion.6), kind=kCustom, calls=%fused_computation.4 | custom fusion | bytes 16793600 | tf_op jit(solution)/shard_map/jit(_take)/gather | solution.py:11
  57.5 25.9 %gather_fusion = f32[4096]{0:T(1024)S(1)} fusion(f32[512]{0:T(512)S(1)} %copy-done.1, s32[4096]{0:T(1024)S(1)} %fusion.6), kind=kCustom, calls=%fused_computation | custom fusion | bytes 49152 | tf_op jit(solution)/shard_map/jit(_take)/gather | solution.py:22
  83.4 0.0 copy-start.6
  83.4 0.0 copy-start.9
  83.5 18.3 %gather_fusion.2 = bf16[4096,1024]{1,0:T(8,128)(2,1)} fusion(bf16[64,1024]{1,0:T(8,128)(2,1)S(1)} %copy.16, s32[4096]{0:T(1024)S(1)} %copy-done.7), kind=kCustom, calls=%fused_computation.2 | custom fusion | bytes 16793600 | tf_op jit(solution)/shard_map/jit(_take)/gather | solution.py:11
  101.7 40.1 %fusion.5 = (f32[4096]{0:T(1024)S(1)}, pred[4096]{0:T(1024)(128)(4,1)S(1)}) fusion(f32[4096]{0:T(1024)S(1)} %gather_fusion, s32[4096]{0:T(1024)S(1)} %copy-done.6, f32[]{:T(128)} %bitcast, f32[]{:T(128)} %bitcast.1, f32[]{:T(128)} %bitcast.2, f32[]{:T(128)} %bitcast.3, f32[]{:T(128)} %bitcast.4, f32[]{:T(128)} %bitcast.5, f32[]{:T(128)} %bitcast.6, ...), kind=kLoop, calls=%fused_computation.19 | loop fusion | flops 581632 | bytes 69888 | tf_op jit(solution)/shard_map/sub | solution.py:36
  141.8 0.0 copy-start.3
  141.8 7.7 %multiply_convert_fusion = bf16[4096,1024]{1,0:T(8,128)(2,1)S(1)} fusion(bf16[4096,1024]{1,0:T(8,128)(2,1)} %gather_fusion.4, bf16[4096,1024]{1,0:T(8,128)(2,1)} %gather_fusion.2, pred[4096]{0:T(1024)(128)(4,1)S(1)} %get-tuple-element.3, pred[4096]{0:T(1024)(128)(4,1)S(1)} %copy-done.10), kind=kLoop, calls=%fused_computation.5 | loop fusion | flops 25165824 | bytes 25174016 | tf_op jit(solution)/shard_map/convert_element_type | solution.py:14
  149.5 3.2 copy-done.2
  152.8 3.1 fusion.13
  155.9 0.0 all-reduce.5.cloned.1.call-update
  155.9 0.0 all-reduce.7.cloned.1.call-start
  156.0 123.6 %all-reduce.5.cloned.1.call-done = f32[1024,128]{1,0:T(8,128)} async-done(((f32[1024,128]{1,0:T(8,128)}), f32[1024,128]{1,0:T(8,128)}) %all-reduce.5.cloned.1.call-update) | async-done | bytes 524304 | tf_op jit(solution)/shard_map/psum | solution.py:31
  279.6 0.0 all-reduce.7.cloned.1.call-update
  279.6 0.2 all-reduce.9.cloned.1.call-start
  279.9 164.3 %all-reduce.7.cloned.1.call-done = f32[1024,128]{1,0:T(8,128)} async-done(((f32[1024,128]{1,0:T(8,128)}), f32[1024,128]{1,0:T(8,128)}) %all-reduce.7.cloned.1.call-update) | async-done | bytes 524304 | tf_op jit(solution)/shard_map/psum | solution.py:31
  444.1 3.3 fusion.14
  447.5 9.1 %fusion.3 = bf16[4096,128]{1,0:T(8,128)(2,1)S(1)} fusion(bf16[4096,1024]{1,0:T(8,128)(2,1)} %copy-done.2, f32[128,1024]{1,0:T(8,128)S(1)} %fusion.14, bf16[4096,128]{1,0:T(8,128)(2,1)S(1)} %copy-done.3, f32[4096]{0:T(1024)S(1)} %get-tuple-element.2), kind=kOutput, calls=%fused_computation.11 | convolution fusion | flops 6445072384 | bytes 11026432 | tf_op jit(solution)/shard_map/dot_general | solution.py:33
  456.6 0.0 copy-start.4
  456.6 1.0 copy-done.4
  457.6 6.6 fusion.15
  464.1 0.0 all-reduce.9.cloned.1.call-update
  464.1 0.3 all-reduce.11.cloned.1.call-start
  464.4 117.9 %all-reduce.9.cloned.1.call-done = f32[1024,128]{1,0:T(8,128)} async-done(((f32[1024,128]{1,0:T(8,128)}), f32[1024,128]{1,0:T(8,128)}) %all-reduce.9.cloned.1.call-update) | async-done | bytes 524304 | tf_op jit(solution)/shard_map/psum | solution.py:31
  582.3 0.0 all-reduce.11.cloned.1.call-update
  582.3 164.4 %all-reduce.11.cloned.1.call-done = f32[1024,128]{1,0:T(8,128)} async-done(((f32[1024,128]{1,0:T(8,128)}), f32[1024,128]{1,0:T(8,128)}) %all-reduce.11.cloned.1.call-update) | async-done | bytes 524304 | tf_op jit(solution)/shard_map/psum | solution.py:31
  746.7 3.3 fusion.16
  750.0 10.2 %fusion.1 = f32[4096,128]{1,0:T(8,128)} fusion(bf16[4096,1024]{1,0:T(8,128)(2,1)} %copy-done.2, f32[128,1024]{1,0:T(8,128)S(1)} %fusion.16, bf16[4096,128]{1,0:T(8,128)(2,1)S(1)} %copy-done.3, bf16[4096,128]{1,0:T(8,128)(2,1)} %copy-done.4, f32[4096]{0:T(1024)S(1)} %get-tuple-element.2), kind=kOutput, calls=%fused_computation.8 | convolution fusion | flops 6445596672 | bytes 13123584 | tf_op jit(solution)/shard_map/dot_general | solution.py:33
  (16 shorter events, 0.0 us)
Async XLA Ops:
  7.2 437.0 %copy-start = (bf16[1024,1024]{1,0:T(8,128)(2,1)S(1)}, bf16[1024,1024]{1,0:T(8,128)(2,1)}, u32[]{:S(2)}) copy-start(bf16[1024,1024]{1,0:T(8,128)(2,1)} %param.16) | copy-start | bytes 6291460
  7.2 272.4 %all-reduce.5.cloned.1.call-start = ((), (), s32[]{:S(2)}) async-start(), calls=%async_computation | async-start | bytes 1048576 | tf_op jit(solution)/shard_map/psum | solution.py:31
  8.8 23.0 %copy-start.11 = (pred[1024]{0:T(1024)(128)(4,1)}, pred[1024]{0:T(1024)(128)(4,1)S(1)}, u32[]{:S(2)}) copy-start(pred[1024]{0:T(1024)(128)(4,1)S(1)} %compare_and_fusion.2) | copy-start | bytes 3076
  19.2 12.5 %copy-start.8 = (s32[4096]{0:T(1024)S(1)}, s32[4096]{0:T(1024)}, u32[]{:S(2)}) copy-start(s32[4096]{0:T(1024)} %param.15) | copy-start | bytes 49156
  19.2 12.5 %copy-start.5 = (bf16[64,2048]{1,0:T(8,128)(2,1)S(1)}, bf16[64,2048]{1,0:T(8,128)(2,1)}, u32[]{:S(2)}) copy-start(bf16[64,2048]{1,0:T(8,128)(2,1)} %param.9) | copy-start | bytes 786436
  39.2 18.3 %copy-start.1 = (f32[512]{0:T(512)S(1)}, f32[512]{0:T(512)}, u32[]{:S(2)}) copy-start(f32[512]{0:T(512)} %param.12) | copy-start | bytes 6148
  57.5 25.9 %copy-start.7 = (s32[4096]{0:T(1024)S(1)}, s32[4096]{0:T(1024)}, u32[]{:S(2)}) copy-start(s32[4096]{0:T(1024)} %fusion.7) | copy-start | bytes 49156
  83.4 18.3 %copy-start.6 = (s32[4096]{0:T(1024)S(1)}, s32[4096]{0:T(1024)}, u32[]{:S(2)}) copy-start(s32[4096]{0:T(1024)} %param.14) | copy-start | bytes 49156
  83.4 18.3 %copy-start.9 = (s32[4096]{0:T(1024)S(1)}, s32[4096]{0:T(1024)}, u32[]{:S(2)}) copy-start(s32[4096]{0:T(1024)} %param.15) | copy-start | bytes 49156
  83.4 58.3 %copy-start.10 = (pred[4096]{0:T(1024)(128)(4,1)S(1)}, pred[4096]{0:T(1024)(128)(4,1)}, u32[]{:S(2)}) copy-start(pred[4096]{0:T(1024)(128)(4,1)} %compare_and_fusion) | copy-start | bytes 12292
  141.8 11.0 %copy-start.3 = (bf16[4096,128]{1,0:T(8,128)(2,1)S(1)}, bf16[4096,128]{1,0:T(8,128)(2,1)}, u32[]{:S(2)}) copy-start(bf16[4096,128]{1,0:T(8,128)(2,1)} %param.17) | copy-start | bytes 3145732
  149.5 3.2 copy-start.2
  155.9 288.2 %all-reduce.7.cloned.1.call-start = ((), (), s32[]{:S(2)}) async-start(), calls=%async_computation.1 | async-start | bytes 1048576 | tf_op jit(solution)/shard_map/psum | solution.py:31
  279.6 302.7 %all-reduce.9.cloned.1.call-start = ((), (), s32[]{:S(2)}) async-start(), calls=%async_computation.2 | async-start | bytes 1048576 | tf_op jit(solution)/shard_map/psum | solution.py:31
  456.6 1.0 copy-start.4
  464.1 282.5 %all-reduce.11.cloned.1.call-start = ((), (), s32[]{:S(2)}) async-start(), calls=%async_computation.3 | async-start | bytes 1048576 | tf_op jit(solution)/shard_map/psum | solution.py:31
Sparse Core Ops, SparseCore 0:
  156.1 123.5 all-reduce.4
  282.2 161.8 all-reduce.6
  464.3 117.9 all-reduce.8
  584.8 161.8 all-reduce.10
